TPU v7x, 32 devices: a whole 2x2x4 slice. The times are simulated.
32 devices in a mesh: rep: 2 (over x), head: 8 (over z, y), seq: 2 (over core).
Axes of the slice: x: 2, y: 2, z: 4, core: 2. Of those that a mesh axis runs over, the one named last changes fastest.
Arguments:
- q_span: bfloat16 [512, 4096], P(('rep', 'head', 'seq')), parts along dimension 0, may hold values from -6 to 6
- k_span: bfloat16 [512, 1024], P(('rep', 'head', 'seq')), parts along dimension 0, may hold values from -6 to 6
- v_span: bfloat16 [512, 1024], P(('rep', 'head', 'seq')), parts along dimension 0, may hold values from -6 to 6
- k_cache: bfloat16 [16, 8192, 128], P(('rep', 'head'), 'seq'), parts along dimension 0, may hold values from -6 to 6
- v_cache: bfloat16 [16, 8192, 128], P(('rep', 'head'), 'seq'), parts along dimension 0, may hold values from -6 to 6
- head_list: int32 [16], P('rep'), parts along dimension 0, may hold values from 0 to 7, each once
- retrieval: int32 [16], P('rep'), parts along dimension 0, may hold values from 0 to 1
- windows: int32 [16], P('rep'), parts along dimension 0, may hold values from 2049 to 4096
- sinks: int32 [16], P('rep'), parts along dimension 0, may hold values from 1 to 64
Outputs:
- attn_out: bfloat16 [512, 4096], P(('rep', 'head', 'seq')), parts along dimension 0
There are 2 independent parts, one for each index of `rep`. A program takes and returns all parts, laid end to end along the dimension named above; each array names one. Nothing has to cross between parts.
Inputs may be any that keep to these rules, and one draw needn't show every extreme that they name: `head_list`: each kv head stands in exactly one slot.
All inputs are finite; a program needn't handle non-finite values.
Results may differ from a plain program's by a relative error of at most 0.0055.
Values may be sent and summed in bfloat16 or wider, within the bound.
No kernel may reach another device: no remote copies, remote signals or barrier semaphores. Data moves between devices by JAX's collectives and lax.ppermute only.
A program may use at most 64 MiB of HBM per device.

v0:
```python
import math

import jax
import jax.numpy as jnp
from jax import lax
from jax.sharding import PartitionSpec as P

KVH = 8


NEG_FILL = -1e30


def absorb(
    running,
    query_rows,
    query_pos,
    key_rows,
    value_rows,
    key_pos,
    is_retrieval,
    window_len,
    sink_len,
    score_scale,
):
    top_score, totals, weighted = running
    scores = jnp.dot(query_rows, key_rows.T, preferred_element_type=jnp.float32) * score_scale
    allowed = (key_pos[None, :] <= query_pos[:, None]) & (
        (is_retrieval == 1)
        | (key_pos[None, :] < sink_len)
        | (key_pos[None, :] > query_pos[:, None] - window_len)
    )
    block_top = jnp.max(jnp.where(allowed, scores, NEG_FILL), axis=1)
    new_top = jnp.maximum(top_score, block_top)
    weights = jnp.where(allowed, jnp.exp(scores - new_top[:, None]), 0.0)
    rescale = jnp.exp(top_score - new_top)
    totals = totals * rescale + jnp.sum(weights, axis=1)
    weighted = weighted * rescale[:, None] + jnp.dot(
        weights.astype(jnp.bfloat16), value_rows, preferred_element_type=jnp.float32
    )
    return (new_top, totals, weighted)


def finish_rows(received, spread, head_list, tok_rows, head_dim):
    top_score, totals, weighted = received
    group_heads = top_score.shape[-1]
    top_score = top_score.reshape(KVH, spread, tok_rows, group_heads)
    totals = totals.reshape(KVH, spread, tok_rows, group_heads)
    weighted = weighted.reshape(KVH, spread, tok_rows, group_heads, head_dim)
    overall = jnp.max(top_score, axis=1, keepdims=True)
    factor = jnp.exp(top_score - overall)
    summed = jnp.sum(totals * factor, axis=1)
    combined = jnp.sum(weighted * factor[..., None], axis=1)
    result = combined / summed[..., None]
    matches = (head_list[:, None] == jnp.arange(KVH, dtype=jnp.int32)[None, :]).astype(jnp.int32)
    inverse = jnp.sum(jnp.arange(KVH, dtype=jnp.int32)[:, None] * matches, axis=0)
    by_group = jnp.take(result, inverse, axis=0)
    return (
        by_group.transpose(1, 0, 2, 3)
        .reshape(tok_rows, KVH * group_heads * head_dim)
        .astype(jnp.bfloat16)
    )


def on_device(q_span, k_span, v_span, k_cache, v_cache, head_list, retrieval, windows, sinks):
    head_count = lax.axis_size("head")
    pair_count = lax.axis_size("seq")
    quarters = head_count // KVH
    tok_rows = q_span.shape[0]
    group_width = q_span.shape[1] // KVH
    head_dim = k_cache.shape[2]
    group_heads = group_width // head_dim
    ctx_dev = k_cache.shape[1]
    total_q = tok_rows * head_count * pair_count
    context = ctx_dev * pair_count * quarters
    head_at = lax.axis_index("head")
    pair_at = lax.axis_index("seq")
    slot_index = head_at // quarters
    quarter = head_at % quarters
    kv_group = jnp.take(head_list, slot_index)
    q_groups = q_span.reshape(tok_rows, KVH, group_width)
    kv_groups = jnp.concatenate(
        [k_span.reshape(tok_rows, KVH, head_dim), v_span.reshape(tok_rows, KVH, head_dim)], axis=2
    )
    targets = jnp.take(head_list, jnp.arange(head_count * pair_count) // pair_count // quarters)
    q_send = jnp.take(q_groups, targets, axis=1)
    kv_send = jnp.take(kv_groups, targets, axis=1)
    q_recv, kv_recv = (
        lax.all_to_all(q_send, ("head", "seq"), split_axis=1, concat_axis=0, tiled=True),
        lax.all_to_all(kv_send, ("head", "seq"), split_axis=1, concat_axis=0, tiled=True),
    )
    queries = q_recv.reshape(total_q, group_width)
    span_kv = kv_recv.reshape(total_q, 2 * head_dim)
    query_rows = queries.reshape(total_q * group_heads, head_dim)
    query_pos = context + jnp.arange(total_q * group_heads, dtype=jnp.int32) // group_heads
    is_retrieval = jnp.take(retrieval, kv_group)
    window_len = jnp.take(windows, kv_group)
    sink_len = jnp.take(sinks, kv_group)
    score_scale = 1.0 / math.sqrt(head_dim)
    row_total = total_q * group_heads
    running = (
        jnp.full((row_total,), NEG_FILL, jnp.float32),
        jnp.zeros((row_total,), jnp.float32),
        jnp.zeros((row_total, head_dim), jnp.float32),
    )
    key_block = min(512, ctx_dev)
    segment = quarter * pair_count + pair_at
    first_key = segment * ctx_dev
    cache_keys = k_cache[0]
    cache_values = v_cache[0]

    def key_step(step_index, state):
        start = step_index * key_block
        key_rows = lax.dynamic_slice_in_dim(cache_keys, start, key_block, 0)
        value_rows = lax.dynamic_slice_in_dim(cache_values, start, key_block, 0)
        key_pos = first_key + start + jnp.arange(key_block, dtype=jnp.int32)
        return absorb(
            state,
            query_rows,
            query_pos,
            key_rows,
            value_rows,
            key_pos,
            is_retrieval,
            window_len,
            sink_len,
            score_scale,
        )

    running = lax.fori_loop(0, ctx_dev // key_block, key_step, running)
    span_piece = total_q // (quarters * pair_count)
    span_start = segment * span_piece
    span_rows = lax.dynamic_slice_in_dim(span_kv, span_start, span_piece, 0)
    span_pos = context + span_start + jnp.arange(span_piece, dtype=jnp.int32)
    top_score, totals, weighted = absorb(
        running,
        query_rows,
        query_pos,
        span_rows[:, :head_dim],
        span_rows[:, head_dim:],
        span_pos,
        is_retrieval,
        window_len,
        sink_len,
        score_scale,
    )
    received = (
        lax.all_to_all(
            top_score.reshape(head_count * pair_count, tok_rows, group_heads),
            ("head", "seq"),
            split_axis=0,
            concat_axis=0,
            tiled=True,
        ),
        lax.all_to_all(
            totals.reshape(head_count * pair_count, tok_rows, group_heads),
            ("head", "seq"),
            split_axis=0,
            concat_axis=0,
            tiled=True,
        ),
        lax.all_to_all(
            weighted.reshape(head_count * pair_count, tok_rows, group_width),
            ("head", "seq"),
            split_axis=0,
            concat_axis=0,
            tiled=True,
        ),
    )
    spread = quarters * pair_count
    return finish_rows(received, spread, head_list, tok_rows, head_dim)


def solution(mesh):
    in_specs = (
        P(("rep", "head", "seq"), None),
        P(("rep", "head", "seq"), None),
        P(("rep", "head", "seq"), None),
        P(("rep", "head"), "seq", None),
        P(("rep", "head"), "seq", None),
        P("rep"),
        P("rep"),
        P("rep"),
        P("rep"),
    )
    out_specs = P(("rep", "head", "seq"), None)
    return jax.shard_map(
        on_device, mesh=mesh, in_specs=in_specs, out_specs=out_specs, check_vma=False
    )
```

profile of v0, /device:TPU:0, one launch (start us, length us, event | category | flops | bytes accessed | tf_op | source)
XLA Modules:
  0.0 108.8 jit_solution(10174010634001487285)
XLA Ops:
  0.1 1.3 %gather_fusion = s32[16]{0:T(128)S(1)} fusion(s32[8]{0:T(128)} %param.16, s32[1024]{0:T(1024)S(1)} %pad_clamp_fusion.2), kind=kCustom, calls=%fused_computation | custom fusion | bytes 192 | tf_op jit(solution)/shard_map/jit(_take)/gather | solution.py:85
  3.7 7.4 %all-to-all-start = ((bf16[16,16,512]{2,0,1:T(8,128)(2,1)}), bf16[16,16,512]{2,0,1:T(8,128)(2,1)S(1)}, u32[]{:S(2)}, u32[]{:S(2)}) async-start(bf16[16,16,512]{2,0,1:T(8,128)(2,1)} %select_bitcast_fusion), calls=%async_computation | async-start | bytes 524288 | tf_op jit(solution)/shard_map/all_to_all | solution.py:89
  17.5 3.7 %all-to-all-done = bf16[16,16,512]{2,0,1:T(8,128)(2,1)S(1)} async-done(((bf16[16,16,512]{2,0,1:T(8,128)(2,1)}), bf16[16,16,512]{2,0,1:T(8,128)(2,1)S(1)}, u32[]{:S(2)}, u32[]{:S(2)}) %all-to-all-start) | async-done | bytes 262176 | tf_op jit(solution)/shard_map/all_to_all | solution.py:89
  21.2 3.5 %all-to-all-start.1 = ((bf16[16,16,256]{2,0,1:T(8,128)(2,1)}), bf16[16,16,256]{2,0,1:T(8,128)(2,1)S(1)}, u32[]{:S(2)}, u32[]{:S(2)}) async-start(bf16[16,16,256]{2,0,1:T(8,128)(2,1)} %select_bitcast_fusion.1), calls=%async_computation.1 | async-start | bytes 262144 | tf_op jit(solution)/shard_map/all_to_all | solution.py:90
  24.9 39.5 %while.25 = (s32[]{:T(128)}, f32[1024]{0:T(1024)S(1)}, f32[1024]{0:T(1024)S(1)}, f32[1024,128]{1,0:T(8,128)S(1)}, s32[]{:T(128)}, /*index=5*/pred[]{:T(512)}, s3...) while((s32[]{:T(128)}, f32[1024]{0:T(1024)S(1)}, ...), condition=%wide.region_4.5_spmd.clone.clone, body=%wide.region_1.4_spmd.clone.clone.sunk | while | flops 280904704 | bytes 7973108 | solution.py:130
  24.9 1.7 %fusion.58 = (f32[1024]{0:T(1024)S(1)}, f32[512,1024]{1,0:T(8,128)S(1)}) fusion(s32[1024]{0:T(1024)S(1)} %get-tuple-element.509, pred[512]{0:T(512)(128)(4,1)S(1)} %compare_or_fusion.3, s32[1024]{0:T(1024)S(1)} %get-tuple-element.510, s32[512]{0:T(512)S(1)} %iota_add_fusion.3, bf16[1024,128]{1,0:T(8,128)(2,1)S(1)} %get-tuple-element.554, ...), kind=kOutput, calls=%fused_computation.7.clone.1 | convolution fusion | flops 137886720 | bytes 2505220 | tf_op jit(solution)/shard_map/while/body/eval_jaxpr/dot_general | solution.py:27
  26.7 0.9 fusion.59
  27.6 2.1 %convolution_add_fusion.3 = f32[1024,128]{1,0:T(8,128)S(1)} fusion(f32[512,1024]{1,0:T(8,128)S(1)} %get-tuple-element.512, f32[1024]{0:T(1024)S(1)} %select_maximum_fusion.2, f32[1024,128]{1,0:T(8,128)S(1)} %get-tuple-element.533, f32[1024]{0:T(1024)S(1)} %get-tuple-element.514, pred[]{:T(512)S(6)} %compare.36, ...), kind=kOutput, calls=%fused_computation.13.clone.1 | convolution fusion | flops 138805248 | bytes 3295749 | tf_op jit(solution)/shard_map/while/body/eval_jaxpr/dot_general | solution.py:38
  29.9 1.7 %fusion.58 = (f32[1024]{0:T(1024)S(1)}, f32[512,1024]{1,0:T(8,128)S(1)}) fusion(s32[1024]{0:T(1024)S(1)} %get-tuple-element.509, pred[512]{0:T(512)(128)(4,1)S(1)} %compare_or_fusion.3, s32[1024]{0:T(1024)S(1)} %get-tuple-element.510, s32[512]{0:T(512)S(1)} %iota_add_fusion.3, bf16[1024,128]{1,0:T(8,128)(2,1)S(1)} %get-tuple-element.554, ...), kind=kOutput, calls=%fused_computation.7.clone.1 | convolution fusion | flops 137886720 | bytes 2505220 | tf_op jit(solution)/shard_map/while/body/eval_jaxpr/dot_general | solution.py:27
  31.6 0.9 fusion.59
  32.6 2.1 %convolution_add_fusion.3 = f32[1024,128]{1,0:T(8,128)S(1)} fusion(f32[512,1024]{1,0:T(8,128)S(1)} %get-tuple-element.512, f32[1024]{0:T(1024)S(1)} %select_maximum_fusion.2, f32[1024,128]{1,0:T(8,128)S(1)} %get-tuple-element.533, f32[1024]{0:T(1024)S(1)} %get-tuple-element.514, pred[]{:T(512)S(6)} %compare.36, ...), kind=kOutput, calls=%fused_computation.13.clone.1 | convolution fusion | flops 138805248 | bytes 3295749 | tf_op jit(solution)/shard_map/while/body/eval_jaxpr/dot_general | solution.py:38
  34.8 1.7 %fusion.58 = (f32[1024]{0:T(1024)S(1)}, f32[512,1024]{1,0:T(8,128)S(1)}) fusion(s32[1024]{0:T(1024)S(1)} %get-tuple-element.509, pred[512]{0:T(512)(128)(4,1)S(1)} %compare_or_fusion.3, s32[1024]{0:T(1024)S(1)} %get-tuple-element.510, s32[512]{0:T(512)S(1)} %iota_add_fusion.3, bf16[1024,128]{1,0:T(8,128)(2,1)S(1)} %get-tuple-element.554, ...), kind=kOutput, calls=%fused_computation.7.clone.1 | convolution fusion | flops 137886720 | bytes 2505220 | tf_op jit(solution)/shard_map/while/body/eval_jaxpr/dot_general | solution.py:27
  36.6 0.9 fusion.59
  37.5 2.1 %convolution_add_fusion.3 = f32[1024,128]{1,0:T(8,128)S(1)} fusion(f32[512,1024]{1,0:T(8,128)S(1)} %get-tuple-element.512, f32[1024]{0:T(1024)S(1)} %select_maximum_fusion.2, f32[1024,128]{1,0:T(8,128)S(1)} %get-tuple-element.533, f32[1024]{0:T(1024)S(1)} %get-tuple-element.514, pred[]{:T(512)S(6)} %compare.36, ...), kind=kOutput, calls=%fused_computation.13.clone.1 | convolution fusion | flops 138805248 | bytes 3295749 | tf_op jit(solution)/shard_map/while/body/eval_jaxpr/dot_general | solution.py:38
  39.7 1.7 %fusion.58 = (f32[1024]{0:T(1024)S(1)}, f32[512,1024]{1,0:T(8,128)S(1)}) fusion(s32[1024]{0:T(1024)S(1)} %get-tuple-element.509, pred[512]{0:T(512)(128)(4,1)S(1)} %compare_or_fusion.3, s32[1024]{0:T(1024)S(1)} %get-tuple-element.510, s32[512]{0:T(512)S(1)} %iota_add_fusion.3, bf16[1024,128]{1,0:T(8,128)(2,1)S(1)} %get-tuple-element.554, ...), kind=kOutput, calls=%fused_computation.7.clone.1 | convolution fusion | flops 137886720 | bytes 2505220 | tf_op jit(solution)/shard_map/while/body/eval_jaxpr/dot_general | solution.py:27
  41.5 0.9 fusion.59
  42.5 2.1 %convolution_add_fusion.3 = f32[1024,128]{1,0:T(8,128)S(1)} fusion(f32[512,1024]{1,0:T(8,128)S(1)} %get-tuple-element.512, f32[1024]{0:T(1024)S(1)} %select_maximum_fusion.2, f32[1024,128]{1,0:T(8,128)S(1)} %get-tuple-element.533, f32[1024]{0:T(1024)S(1)} %get-tuple-element.514, pred[]{:T(512)S(6)} %compare.36, ...), kind=kOutput, calls=%fused_computation.13.clone.1 | convolution fusion | flops 138805248 | bytes 3295749 | tf_op jit(solution)/shard_map/while/body/eval_jaxpr/dot_general | solution.py:38
  44.7 1.7 %fusion.58 = (f32[1024]{0:T(1024)S(1)}, f32[512,1024]{1,0:T(8,128)S(1)}) fusion(s32[1024]{0:T(1024)S(1)} %get-tuple-element.509, pred[512]{0:T(512)(128)(4,1)S(1)} %compare_or_fusion.3, s32[1024]{0:T(1024)S(1)} %get-tuple-element.510, s32[512]{0:T(512)S(1)} %iota_add_fusion.3, bf16[1024,128]{1,0:T(8,128)(2,1)S(1)} %get-tuple-element.554, ...), kind=kOutput, calls=%fused_computation.7.clone.1 | convolution fusion | flops 137886720 | bytes 2505220 | tf_op jit(solution)/shard_map/while/body/eval_jaxpr/dot_general | solution.py:27
  46.4 0.9 fusion.59
  47.4 2.1 %convolution_add_fusion.3 = f32[1024,128]{1,0:T(8,128)S(1)} fusion(f32[512,1024]{1,0:T(8,128)S(1)} %get-tuple-element.512, f32[1024]{0:T(1024)S(1)} %select_maximum_fusion.2, f32[1024,128]{1,0:T(8,128)S(1)} %get-tuple-element.533, f32[1024]{0:T(1024)S(1)} %get-tuple-element.514, pred[]{:T(512)S(6)} %compare.36, ...), kind=kOutput, calls=%fused_computation.13.clone.1 | convolution fusion | flops 138805248 | bytes 3295749 | tf_op jit(solution)/shard_map/while/body/eval_jaxpr/dot_general | solution.py:38
  49.6 1.7 %fusion.58 = (f32[1024]{0:T(1024)S(1)}, f32[512,1024]{1,0:T(8,128)S(1)}) fusion(s32[1024]{0:T(1024)S(1)} %get-tuple-element.509, pred[512]{0:T(512)(128)(4,1)S(1)} %compare_or_fusion.3, s32[1024]{0:T(1024)S(1)} %get-tuple-element.510, s32[512]{0:T(512)S(1)} %iota_add_fusion.3, bf16[1024,128]{1,0:T(8,128)(2,1)S(1)} %get-tuple-element.554, ...), kind=kOutput, calls=%fused_computation.7.clone.1 | convolution fusion | flops 137886720 | bytes 2505220 | tf_op jit(solution)/shard_map/while/body/eval_jaxpr/dot_general | solution.py:27
  52.3 2.1 %convolution_add_fusion.3 = f32[1024,128]{1,0:T(8,128)S(1)} fusion(f32[512,1024]{1,0:T(8,128)S(1)} %get-tuple-element.512, f32[1024]{0:T(1024)S(1)} %select_maximum_fusion.2, f32[1024,128]{1,0:T(8,128)S(1)} %get-tuple-element.533, f32[1024]{0:T(1024)S(1)} %get-tuple-element.514, pred[]{:T(512)S(6)} %compare.36, ...), kind=kOutput, calls=%fused_computation.13.clone.1 | convolution fusion | flops 138805248 | bytes 3295749 | tf_op jit(solution)/shard_map/while/body/eval_jaxpr/dot_general | solution.py:38
  54.6 1.7 %fusion.58 = (f32[1024]{0:T(1024)S(1)}, f32[512,1024]{1,0:T(8,128)S(1)}) fusion(s32[1024]{0:T(1024)S(1)} %get-tuple-element.509, pred[512]{0:T(512)(128)(4,1)S(1)} %compare_or_fusion.3, s32[1024]{0:T(1024)S(1)} %get-tuple-element.510, s32[512]{0:T(512)S(1)} %iota_add_fusion.3, bf16[1024,128]{1,0:T(8,128)(2,1)S(1)} %get-tuple-element.554, ...), kind=kOutput, calls=%fused_computation.7.clone.1 | convolution fusion | flops 137886720 | bytes 2505220 | tf_op jit(solution)/shard_map/while/body/eval_jaxpr/dot_general | solution.py:27
  57.3 2.1 %convolution_add_fusion.3 = f32[1024,128]{1,0:T(8,128)S(1)} fusion(f32[512,1024]{1,0:T(8,128)S(1)} %get-tuple-element.512, f32[1024]{0:T(1024)S(1)} %select_maximum_fusion.2, f32[1024,128]{1,0:T(8,128)S(1)} %get-tuple-element.533, f32[1024]{0:T(1024)S(1)} %get-tuple-element.514, pred[]{:T(512)S(6)} %compare.36, ...), kind=kOutput, calls=%fused_computation.13.clone.1 | convolution fusion | flops 138805248 | bytes 3295749 | tf_op jit(solution)/shard_map/while/body/eval_jaxpr/dot_general | solution.py:38
  59.5 1.7 %fusion.58 = (f32[1024]{0:T(1024)S(1)}, f32[512,1024]{1,0:T(8,128)S(1)}) fusion(s32[1024]{0:T(1024)S(1)} %get-tuple-element.509, pred[512]{0:T(512)(128)(4,1)S(1)} %compare_or_fusion.3, s32[1024]{0:T(1024)S(1)} %get-tuple-element.510, s32[512]{0:T(512)S(1)} %iota_add_fusion.3, bf16[1024,128]{1,0:T(8,128)(2,1)S(1)} %get-tuple-element.554, ...), kind=kOutput, calls=%fused_computation.7.clone.1 | convolution fusion | flops 137886720 | bytes 2505220 | tf_op jit(solution)/shard_map/while/body/eval_jaxpr/dot_general | solution.py:27
  62.2 2.1 %convolution_add_fusion.3 = f32[1024,128]{1,0:T(8,128)S(1)} fusion(f32[512,1024]{1,0:T(8,128)S(1)} %get-tuple-element.512, f32[1024]{0:T(1024)S(1)} %select_maximum_fusion.2, f32[1024,128]{1,0:T(8,128)S(1)} %get-tuple-element.533, f32[1024]{0:T(1024)S(1)} %get-tuple-element.514, pred[]{:T(512)S(6)} %compare.36, ...), kind=kOutput, calls=%fused_computation.13.clone.1 | convolution fusion | flops 138805248 | bytes 3295749 | tf_op jit(solution)/shard_map/while/body/eval_jaxpr/dot_general | solution.py:38
  65.9 6.0 %all-to-all-start.4 = ((f32[16,16,4]{1,2,0:T(4,128)}), f32[16,16,4]{1,2,0:T(4,128)S(1)}, u32[]{:S(2)}, u32[]{:S(2)}) async-start(f32[16,16,4]{1,2,0:T(4,128)} %copy.67), calls=%async_computation.4 | async-start | bytes 65536 | tf_op jit(solution)/shard_map/all_to_all | solution.py:155
  72.8 5.7 %all-to-all-done.4 = f32[16,16,4]{1,2,0:T(4,128)S(1)} async-done(((f32[16,16,4]{1,2,0:T(4,128)}), f32[16,16,4]{1,2,0:T(4,128)S(1)}, u32[]{:S(2)}, u32[]{:S(2)}) %all-to-all-start.4) | async-done | bytes 4128 | tf_op jit(solution)/shard_map/all_to_all | solution.py:155
  78.5 3.5 %all-to-all-start.3 = ((f32[16,16,4]{1,2,0:T(4,128)}), f32[16,16,4]{1,2,0:T(4,128)S(1)}, u32[]{:S(2)}, u32[]{:S(2)}) async-start(f32[16,16,4]{1,2,0:T(4,128)} %copy.61), calls=%async_computation.3 | async-start | bytes 65536 | tf_op jit(solution)/shard_map/all_to_all | solution.py:148
  83.4 5.2 %all-to-all-done.3 = f32[16,16,4]{1,2,0:T(4,128)S(1)} async-done(((f32[16,16,4]{1,2,0:T(4,128)}), f32[16,16,4]{1,2,0:T(4,128)S(1)}, u32[]{:S(2)}, u32[]{:S(2)}) %all-to-all-start.3) | async-done | bytes 4128 | tf_op jit(solution)/shard_map/all_to_all | solution.py:148
  88.6 3.6 %all-to-all-start.2 = ((f32[16,16,512]{2,1,0:T(8,128)}), f32[16,16,512]{2,1,0:T(8,128)S(1)}, u32[]{:S(2)}, u32[]{:S(2)}) async-start(f32[16,16,512]{2,1,0:T(8,128)} %reshape.197), calls=%async_computation.2 | async-start | bytes 1048576 | tf_op jit(solution)/shard_map/all_to_all | solution.py:162
  92.6 14.0 %all-to-all-done.2 = f32[16,16,512]{2,1,0:T(8,128)S(1)} async-done(((f32[16,16,512]{2,1,0:T(8,128)}), f32[16,16,512]{2,1,0:T(8,128)S(1)}, u32[]{:S(2)}, u32[]{:S(2)}) %all-to-all-start.2) | async-done | bytes 524320 | tf_op jit(solution)/shard_map/all_to_all | solution.py:162
  (113 shorter events, 15.6 us)
Async XLA Ops:
  0.0 11.1 %copy-start = (bf16[16,1024]{1,0:T(8,128)(2,1)S(1)}, bf16[16,1024]{1,0:T(8,128)(2,1)}, u32[]{:S(2)}) copy-start(bf16[16,1024]{1,0:T(8,128)(2,1)} %param.12) | copy-start | bytes 98308
  0.0 11.2 %copy-start.1 = (s32[8]{0:T(128)S(1)}, s32[8]{0:T(128)}, u32[]{:S(2)}) copy-start(s32[8]{0:T(128)} %param.16) | copy-start | bytes 100
  0.0 11.1 %copy-start.2 = (bf16[16,1024]{1,0:T(8,128)(2,1)S(1)}, bf16[16,1024]{1,0:T(8,128)(2,1)}, u32[]{:S(2)}) copy-start(bf16[16,1024]{1,0:T(8,128)(2,1)} %param.13) | copy-start | bytes 98308
  0.0 12.3 %copy-start.3 = (s32[8]{0:T(128)S(1)}, s32[8]{0:T(128)}, u32[]{:S(2)}) copy-start(s32[8]{0:T(128)} %param.17) | copy-start | bytes 100
  0.0 13.0 %copy-start.4 = (s32[8]{0:T(128)S(1)}, s32[8]{0:T(128)}, u32[]{:S(2)}) copy-start(s32[8]{0:T(128)} %param.19) | copy-start | bytes 100
  0.0 14.8 %copy-start.5 = (s32[8]{0:T(128)S(1)}, s32[8]{0:T(128)}, u32[]{:S(2)}) copy-start(s32[8]{0:T(128)} %param.18) | copy-start | bytes 100
  3.7 17.4 %all-to-all-start = ((bf16[16,16,512]{2,0,1:T(8,128)(2,1)}), bf16[16,16,512]{2,0,1:T(8,128)(2,1)S(1)}, u32[]{:S(2)}, u32[]{:S(2)}) async-start(bf16[16,16,512]{2,0,1:T(8,128)(2,1)} %select_bitcast_fusion), calls=%async_computation | async-start | bytes 524288 | tf_op jit(solution)/shard_map/all_to_all | solution.py:89
  21.2 43.2 %all-to-all-start.1 = ((bf16[16,16,256]{2,0,1:T(8,128)(2,1)}), bf16[16,16,256]{2,0,1:T(8,128)(2,1)S(1)}, u32[]{:S(2)}, u32[]{:S(2)}) async-start(bf16[16,16,256]{2,0,1:T(8,128)(2,1)} %select_bitcast_fusion.1), calls=%async_computation.1 | async-start | bytes 262144 | tf_op jit(solution)/shard_map/all_to_all | solution.py:90
  65.9 12.6 %all-to-all-start.4 = ((f32[16,16,4]{1,2,0:T(4,128)}), f32[16,16,4]{1,2,0:T(4,128)S(1)}, u32[]{:S(2)}, u32[]{:S(2)}) async-start(f32[16,16,4]{1,2,0:T(4,128)} %copy.67), calls=%async_computation.4 | async-start | bytes 65536 | tf_op jit(solution)/shard_map/all_to_all | solution.py:155
  78.5 10.1 %all-to-all-start.3 = ((f32[16,16,4]{1,2,0:T(4,128)}), f32[16,16,4]{1,2,0:T(4,128)S(1)}, u32[]{:S(2)}, u32[]{:S(2)}) async-start(f32[16,16,4]{1,2,0:T(4,128)} %copy.61), calls=%async_computation.3 | async-start | bytes 65536 | tf_op jit(solution)/shard_map/all_to_all | solution.py:148
  88.6 18.0 %all-to-all-start.2 = ((f32[16,16,512]{2,1,0:T(8,128)}), f32[16,16,512]{2,1,0:T(8,128)S(1)}, u32[]{:S(2)}, u32[]{:S(2)}) async-start(f32[16,16,512]{2,1,0:T(8,128)} %reshape.197), calls=%async_computation.2 | async-start | bytes 1048576 | tf_op jit(solution)/shard_map/all_to_all | solution.py:162
where the time goes:
time: 110 us; the launch traced here: 109 us
  matrix products  31.8 us (29%)
  waiting for transfers between devices  28.7 us (26%)
  starting transfers between devices  23.9 us (22%)
  local copies, waits for them, and re-layouts  10.4 us (9%)
  other arithmetic  10.4 us (9%)
  between operations  2.82 us (3%)
    dot_general x9, matrix products, absorb(): jnp.dot(weights.astype(jnp.bfloat16), value_rows, preferred_element_type=...  17.6 us
    dot_general x9, matrix products, absorb(): jnp.dot(query_rows, key_rows.T, preferred_element_type=jnp.float32)  14.2 us
    all_to_all x1, waiting for transfers between devices, on_device(): lax.all_to_all(weighted.reshape(head_count * pair_count, tok_rows, group_...  14 us
    reduce_sum x9, other arithmetic, absorb(): totals = totals * rescale + jnp.sum(weights, axis=1)  7.68 us
    all_to_all x1, starting transfers between devices, on_device(): lax.all_to_all(q_send, ('head', 'seq'), split_axis=1, concat_axis=0, tile...  7.39 us
    all_to_all x1, starting transfers between devices, on_device(): lax.all_to_all(totals.reshape(head_count * pair_count, tok_rows, group_he...  5.96 us
    all_to_all x1, waiting for transfers between devices, on_device(): lax.all_to_all(totals.reshape(head_count * pair_count, tok_rows, group_he...  5.73 us
    all_to_all x1, waiting for transfers between devices, on_device(): lax.all_to_all(top_score.reshape(head_count * pair_count, tok_rows, group...  5.25 us
  transfers between devices with their start and end apart: 5, of which 4 were waited for; matrix products, arithmetic and copies ran while one was open for 42% of the time, Pallas kernels for 0%

commit v1 on v0

--- a/solution.py
+++ b/solution.py
@@ -1,8 +1,11 @@
+import functools
 import math
 
 import jax
 import jax.numpy as jnp
 from jax import lax
+from jax.experimental import pallas as pl
+from jax.experimental.pallas import tpu as pltpu
 from jax.sharding import PartitionSpec as P
 
 KVH = 8
@@ -62,7 +65,7 @@
     )
 
 
-def on_device(q_span, k_span, v_span, k_cache, v_cache, head_list, retrieval, windows, sinks):
+def on_device_quarters(q_span, k_span, v_span, k_cache, v_cache, head_list, retrieval, windows, sinks):
     head_count = lax.axis_size("head")
     pair_count = lax.axis_size("seq")
     quarters = head_count // KVH
@@ -171,7 +174,281 @@
     return finish_rows(received, spread, head_list, tok_rows, head_dim)
 
 
+VMEM_SPEC = pl.BlockSpec(memory_space=pltpu.VMEM)
+SMEM_SPEC = pl.BlockSpec(memory_space=pltpu.SMEM)
+
+
+def pack_kernel(head_ref, q_ref, k_ref, v_ref, out_ref, *, group_width, head_dim):
+    for slot in range(out_ref.shape[0]):
+        group = head_ref[slot]
+        q_start = pl.multiple_of(group * group_width, 128)
+        kv_start = pl.multiple_of(group * head_dim, 128)
+        out_ref[slot, :, :group_width] = q_ref[:, pl.ds(q_start, group_width)]
+        out_ref[slot, :, group_width : group_width + head_dim] = k_ref[:, pl.ds(kv_start, head_dim)]
+        out_ref[slot, :, group_width + head_dim :] = v_ref[:, pl.ds(kv_start, head_dim)]
+
+
+def unpack_kernel(head_ref, in_ref, out_ref):
+    width = in_ref.shape[2]
+    for slot in range(in_ref.shape[0]):
+        start = pl.multiple_of(head_ref[slot] * width, 128)
+        out_ref[:, pl.ds(start, width)] = in_ref[slot]
+
+
+def attend_kernel(
+    head_ref,
+    retrieval_ref,
+    window_ref,
+    sink_ref,
+    recv_ref,
+    peer_ref,
+    k_peer,
+    v_peer,
+    k_source,
+    v_source,
+    out_ref,
+    k_own,
+    v_own,
+    score_ref,
+    top_ref,
+    total_ref,
+    acc_ref,
+    own_sem,
+    *,
+    tok_rows,
+    group_heads,
+    head_dim,
+    key_block,
+    row_block,
+):
+    k_copy = pltpu.make_async_copy(k_source, k_own, own_sem.at[0])
+    v_copy = pltpu.make_async_copy(v_source, v_own, own_sem.at[1])
+    k_copy.start()
+    v_copy.start()
+    pair_at = lax.axis_index("seq")
+    kv_group = head_ref[lax.axis_index("head")]
+    is_retrieval = retrieval_ref[kv_group]
+    window_len = window_ref[kv_group]
+    sink_len = sink_ref[kv_group]
+    tokens = recv_ref.shape[0]
+    rows = tokens * group_heads
+    group_width = group_heads * head_dim
+    ctx_dev = k_own.shape[0]
+    context = 2 * ctx_dev
+    f32, bf16 = jnp.float32, jnp.bfloat16
+    scale = math.log2(math.e) / math.sqrt(head_dim)
+
+    def token_pos(index, pair):
+        return context + ((index // tok_rows) * 2 + pair) * tok_rows + index % tok_rows
+
+    queries = jnp.concatenate(
+        [recv_ref[:, k * head_dim : (k + 1) * head_dim] for k in range(group_heads)], axis=0
+    )
+    scaled = queries.astype(f32) * scale
+    high = scaled.astype(bf16)
+    low = (scaled - high.astype(f32)).astype(bf16)
+    queries = jnp.concatenate([high, low], axis=1)
+    row_token = lax.broadcasted_iota(jnp.int32, (1, rows), 1) % tokens
+    query_pos = token_pos(row_token, pair_at)
+
+    span_k = pl.ds(group_width, head_dim)
+    span_v = pl.ds(group_width + head_dim, head_dim)
+    cached, spans = [], []
+    for k_ref, v_ref, pair in ((k_peer, v_peer, 1 - pair_at), (k_own, v_own, pair_at)):
+        for start in range(0, ctx_dev, key_block):
+            cached.append((k_ref, v_ref, start, key_block, pair))
+    for ref, pair in ((recv_ref, pair_at), (peer_ref, 1 - pair_at)):
+        spans.append((ref, pair))
+
+    def load_keys(index):
+        if index < len(cached):
+            k_ref, _, start, size, _ = cached[index]
+            return k_ref[start : start + size, :]
+        return spans[index - len(cached)][0][:, span_k]
+
+    def load_values(index):
+        if index < len(cached):
+            _, v_ref, start, size, _ = cached[index]
+            return v_ref[start : start + size, :]
+        return spans[index - len(cached)][0][:, span_v]
+
+    def place(index):
+        if index < len(cached):
+            return index * key_block, key_block
+        return len(cached) * key_block + (index - len(cached)) * tokens, tokens
+
+    def first_pos(index):
+        _, _, start, _, pair = cached[index]
+        return pair * ctx_dev + start
+
+    def scores(index, row_at, masked):
+        keys = load_keys(index)
+        keys = jnp.concatenate([keys, keys], axis=1)
+        block = lax.dot_general(
+            keys,
+            queries[row_at : row_at + row_block],
+            (((1,), (1,)), ((), ())),
+            preferred_element_type=f32,
+        )
+        size = block.shape[0]
+        pos_q = query_pos[:, row_at : row_at + row_block]
+        column = lax.broadcasted_iota(jnp.int32, (size, 1), 0)
+        allowed = None
+        if index >= len(cached):
+            pos_k = token_pos(column, spans[index - len(cached)][1])
+            allowed = pos_k <= pos_q
+        else:
+            pos_k = first_pos(index) + column
+        if masked:
+            near = (pos_k < sink_len) | (pos_k > pos_q - window_len)
+            allowed = near if allowed is None else allowed & near
+        if allowed is not None:
+            block = jnp.where(allowed, block, NEG_FILL)
+        start, _ = place(index)
+        score_ref[start : start + size, row_at : row_at + row_block] = block
+        return jnp.max(block.reshape(size // 8, 8, row_block), axis=0)
+
+    def weighted(index, row_at, top):
+        start, size = place(index)
+        block = score_ref[start : start + size, row_at : row_at + row_block]
+        weights = jnp.exp2(block - top)
+        total = jnp.sum(weights.reshape(size // 8, 8, row_block), axis=0)
+        acc = lax.dot_general(
+            load_values(index),
+            weights.astype(bf16),
+            (((0,), (0,)), ((), ())),
+            preferred_element_type=f32,
+        )
+        return total, acc
+
+    def finish(row_at, total, acc):
+        result = (acc / jnp.sum(total, axis=0, keepdims=True)).T.astype(bf16)
+        for start in range(0, row_block, tokens):
+            head = (row_at + start) // tokens
+            out_ref[:, head * head_dim : (head + 1) * head_dim] = result[start : start + tokens]
+
+    blocks = len(cached) + len(spans)
+    row_starts = list(range(0, rows, row_block))
+
+    @pl.when(is_retrieval == 1)
+    def _():
+        tops = {}
+        for step in range(len(row_starts) + 1):
+            running, total, acc = None, None, None
+            for index in range(blocks):
+                if step == 0 and index == len(cached) // 2:
+                    k_copy.wait()
+                if step < len(row_starts):
+                    top = scores(index, row_starts[step], False)
+                    running = top if running is None else jnp.maximum(running, top)
+                if step == 1 and index == 0:
+                    v_copy.wait()
+                if step > 0:
+                    part_total, part_acc = weighted(index, row_starts[step - 1], tops[step - 1])
+                    total = part_total if total is None else total + part_total
+                    acc = part_acc if acc is None else acc + part_acc
+            if step < len(row_starts):
+                tops[step] = jnp.max(running, axis=0, keepdims=True)
+            if step > 0:
+                finish(row_starts[step - 1], total, acc)
+
+    @pl.when(is_retrieval != 1)
+    def _():
+        k_copy.wait()
+        v_copy.wait()
+
+        def needed(index):
+            pos = first_pos(index)
+            return (pos < sink_len) | (pos + key_block - 1 > context - window_len)
+
+        top_ref[...] = jnp.full(top_ref.shape, NEG_FILL, f32)
+        total_ref[...] = jnp.zeros(total_ref.shape, f32)
+        acc_ref[...] = jnp.zeros(acc_ref.shape, f32)
+
+        def first(index):
+            for row_at in row_starts:
+                cols = slice(row_at, row_at + row_block)
+                top_ref[:, cols] = jnp.maximum(top_ref[:, cols], scores(index, row_at, True))
+
+        def second(index):
+            for row_at in row_starts:
+                cols = slice(row_at, row_at + row_block)
+                top = jnp.max(top_ref[:, cols], axis=0, keepdims=True)
+                total, acc = weighted(index, row_at, top)
+                total_ref[:, cols] += total
+                acc_ref[:, cols] += acc
+
+        for work in (first, second):
+            for index in range(blocks):
+                if index < len(cached):
+                    pl.when(needed(index))(functools.partial(work, index))
+                else:
+                    work(index)
+        for row_at in row_starts:
+            cols = slice(row_at, row_at + row_block)
+            finish(row_at, total_ref[:, cols], acc_ref[:, cols])
+
+
+def on_device_pairs(q_span, k_span, v_span, k_cache, v_cache, head_list, retrieval, windows, sinks):
+    head_count = lax.axis_size("head")
+    tok_rows = q_span.shape[0]
+    group_width = q_span.shape[1] // KVH
+    head_dim = k_cache.shape[2]
+    group_heads = group_width // head_dim
+    ctx_dev = k_cache.shape[1]
+    tokens = tok_rows * head_count
+    rows = tokens * group_heads
+    swap = [(0, 1), (1, 0)]
+    k_own, v_own = k_cache[0], v_cache[0]
+    k_peer = lax.ppermute(k_own, "seq", swap)
+    v_peer = lax.ppermute(v_own, "seq", swap)
+    send = pl.pallas_call(
+        functools.partial(pack_kernel, group_width=group_width, head_dim=head_dim),
+        out_shape=jax.ShapeDtypeStruct((head_count, tok_rows, group_width + 2 * head_dim), jnp.bfloat16),
+        in_specs=[SMEM_SPEC, VMEM_SPEC, VMEM_SPEC, VMEM_SPEC],
+        out_specs=VMEM_SPEC,
+    )(head_list, q_span, k_span, v_span)
+    recv = lax.all_to_all(send, "head", split_axis=0, concat_axis=0, tiled=True)
+    recv = recv.reshape(tokens, group_width + 2 * head_dim)
+    peer = lax.ppermute(recv, "seq", swap)
+    key_block = math.gcd(ctx_dev, 1024)
+    row_block = 256
+    keys = 2 * ctx_dev + 2 * tokens
+    result = pl.pallas_call(
+        functools.partial(
+            attend_kernel,
+            tok_rows=tok_rows,
+            group_heads=group_heads,
+            head_dim=head_dim,
+            key_block=key_block,
+            row_block=row_block,
+        ),
+        out_shape=jax.ShapeDtypeStruct((tokens, group_width), jnp.bfloat16),
+        in_specs=[SMEM_SPEC] * 4 + [VMEM_SPEC] * 4 + [pl.BlockSpec(memory_space=pltpu.HBM)] * 2,
+        out_specs=VMEM_SPEC,
+        scratch_shapes=[
+            pltpu.VMEM((ctx_dev, head_dim), jnp.bfloat16),
+            pltpu.VMEM((ctx_dev, head_dim), jnp.bfloat16),
+            pltpu.VMEM((keys, rows), jnp.float32),
+            pltpu.VMEM((8, rows), jnp.float32),
+            pltpu.VMEM((8, rows), jnp.float32),
+            pltpu.VMEM((head_dim, rows), jnp.float32),
+            pltpu.SemaphoreType.DMA((2,)),
+        ],
+        compiler_params=pltpu.CompilerParams(vmem_limit_bytes=40 * 2**20),
+    )(head_list, retrieval, windows, sinks, recv, peer, k_peer, v_peer, k_own, v_own)
+    result = result.reshape(head_count, tok_rows, group_width)
+    back = lax.all_to_all(result, "head", split_axis=0, concat_axis=0, tiled=True)
+    return pl.pallas_call(
+        unpack_kernel,
+        out_shape=jax.ShapeDtypeStruct((tok_rows, KVH * group_width), jnp.bfloat16),
+        in_specs=[SMEM_SPEC, VMEM_SPEC],
+        out_specs=VMEM_SPEC,
+    )(head_list, back)
+
+
 def solution(mesh):
+    on_device = on_device_pairs if mesh.shape["head"] == KVH else on_device_quarters
     in_specs = (
         P(("rep", "head", "seq"), None),
         P(("rep", "head", "seq"), None),

time: 110 us -> 40.5 us (0.37)
  matrix products: 31.8 us -> 0 us
  waiting for transfers between devices: 28.7 us -> 1.44 us
  blocking collectives: 0 us -> 26.2 us
  starting transfers between devices: 23.9 us -> 0.51 us
  other arithmetic: 10.4 us -> 0 us
  Pallas kernels: 0 us -> 9.55 us
  local copies, waits for them, and re-layouts: 10.4 us -> 2.46 us
  between operations: 2.82 us -> 0.06 us
    dot_general x18 -> x0, matrix products: 31.8 us -> none  [the longest x9 17.6 us: absorb(): jnp.dot(weights.astype(jnp.bfloat16), value_rows, preferred_element_type=...]
    all_to_all x5 -> x0, waiting for transfers between devices: 28.7 us -> none  [the longest x1 14 us: on_device(): lax.all_to_all(weighted.reshape(head_count * pair_count, tok_rows, group_...]
    all_to_all x0 -> x2, blocking collectives: none -> 26.2 us  [the longest x1 15.5 us: on_device_pairs(): recv = lax.all_to_all(send, 'head', split_axis=0, concat_axis=0, tiled=True)]
    all_to_all x5 -> x0, starting transfers between devices: 23.9 us -> none  [the longest x1 7.39 us: on_device(): lax.all_to_all(q_send, ('head', 'seq'), split_axis=1, concat_axis=0, tile...]
    pallas_call x0 -> x3, Pallas kernels: none -> 9.55 us  [the longest x1 6.33 us: on_device_pairs(): pl.pallas_call(functools.partial(attend_kernel, tok_rows=tok_rows, group_...]
    reduce_sum x12 -> x0, other arithmetic: 8.19 us -> none  [the longest x9 7.68 us: absorb(): totals = totals * rescale + jnp.sum(weights, axis=1)]
    reshape x8 -> x0, local copies, waits for them, and re-layouts: 3.78 us -> none  [the longest x1 0.92 us: on_device(): q_groups = q_span.reshape(tok_rows, KVH, group_width)]
    gather x4 -> x0, local copies, waits for them, and re-layouts: 3.02 us -> none  [the longest x1 1.33 us: on_device(): jnp.take(head_list, jnp.arange(head_count * pair_count) // pair_count //...]
  transfers between devices with their start and end apart: 5 -> 3, of which waited for: 4 -> 1; matrix products, arithmetic and copies ran while one was open for 42% -> 0% of each run, Pallas kernels for 0% -> 4%
where the time goes in v1:
time: 40.5 us; the launch traced here: 40.2 us
  blocking collectives  26.2 us (65%)
  Pallas kernels  9.55 us (24%)
  local copies, waits for them, and re-layouts  2.46 us (6%)
  waiting for transfers between devices  1.44 us (4%)
  starting transfers between devices  0.51 us (1%)
    all_to_all x1, blocking collectives, on_device_pairs(): recv = lax.all_to_all(send, 'head', split_axis=0, concat_axis=0, tiled=True)  15.5 us
    all_to_all x1, blocking collectives, on_device_pairs(): lax.all_to_all(result, 'head', split_axis=0, concat_axis=0, tiled=True)  10.6 us
    pallas_call x1, Pallas kernels, on_device_pairs(): pl.pallas_call(functools.partial(attend_kernel, tok_rows=tok_rows, group_...  6.33 us
    unnamed x12, local copies, waits for them, and re-layouts  2.46 us
    pallas_call x1, Pallas kernels, on_device_pairs(): pl.pallas_call(functools.partial(pack_kernel, group_width=group_width, he...  1.63 us
    pallas_call x1, Pallas kernels, on_device_pairs(): pl.pallas_call(unpack_kernel, out_shape=jax.ShapeDtypeStruct((tok_rows, K...  1.58 us
    ppermute x1, waiting for transfers between devices, on_device_pairs(): peer = lax.ppermute(recv, 'seq', swap)  1.43 us
  transfers between devices with their start and end apart: 3, of which 1 were waited for; matrix products, arithmetic and copies ran while one was open for 0% of the time, Pallas kernels for 4%

profile of v1, /device:TPU:0, one launch (start us, length us, event | category | flops | bytes accessed | tf_op | source)
XLA Modules:
  0.0 40.2 jit_solution(2969697271176242601)
XLA Ops:
  0.0 0.5 %collective-permute-start.1 = (bf16[4096,128]{1,0:T(8,128)(2,1)}, bf16[4096,128]{1,0:T(8,128)(2,1)S(1)}, u32[]{:S(2)}, u32[]{:S(2)}) collective-permute-start(bf16[4096,128]{1,0:T(8,128)(2,1)} %bitcast.4), channel_id=1, source_target_pairs={{0,1},{1,0},{2,3},{3,2},{4,5},{5,4},{6,7},{7,6},{8,9},{9,8},{10,11... | collective-permute-start | bytes 3145736 | tf_op jit(solution)/shard_map/ppermute | solution.py:403
  0.5 0.1 collective-permute-start.2
  0.5 1.6 %shard_map.91 = bf16[8,16,768]{2,1,0:T(8,128)(2,1)} custom-call(s32[8]{0:T(128)} %head_ref.5, bf16[16,4096]{1,0:T(8,128)(2,1)} %q_ref.1, bf16[16,1024]{1,0:T(8,128)(2,1)} %k_ref.1, bf16[16,1024]{1,0:T(8,128)(2,1)} %v_ref.1), custom_call_target="tpu_custom_call" | custom-call | tf_op jit(solution)/shard_map/pallas_call | solution.py:405
  2.1 0.0 copy-start.5
  2.1 15.5 %all_to_all.10 = bf16[8,16,768]{2,1,0:T(8,128)(2,1)S(1)} all-to-all(bf16[8,16,768]{2,1,0:T(8,128)(2,1)} %shard_map.91), channel_id=1, replica_groups=mesh['rep'=2,'head'=8,'seq'=2] {'head'}, dimensions={0} | all-to-all | bytes 393216 | tf_op jit(solution)/shard_map/all_to_all | solution.py:411
  17.7 0.0 copy-start.2
  17.7 0.0 copy-start.3
  17.7 0.0 copy-start.4
  17.7 0.0 collective-permute-start
  17.7 1.4 %collective-permute-done.peer_ref = bf16[128,768]{1,0:T(8,128)(2,1)S(1)} collective-permute-done((bf16[128,768]{1,0:T(8,128)(2,1)S(1)}, bf16[128,768]{1,0:T(8,128)(2,1)S(1)}, u32[]{:S(2)}, u32[]{:S(2)}) %collective-permute-start) | collective-permute-done | bytes 196640 | tf_op jit(solution)/shard_map/ppermute | solution.py:413
  19.1 0.0 collective-permute-done.1.k_peer
  19.1 0.0 collective-permute-done.2.v_peer
  19.1 0.0 copy-done.5
  19.1 0.0 copy-done.2
  19.1 0.0 copy-done.3
  19.2 0.0 copy-done.4
  19.2 0.0 copy-start
  19.2 1.2 %copy-done = bf16[1,4096,128]{2,1,0:T(8,128)(2,1)S(1)} copy-done((bf16[1,4096,128]{2,1,0:T(8,128)(2,1)S(1)}, bf16[1,4096,128]{2,1,0:T(8,128)(2,1)}, u32[]{:S(2)}) %copy-start) | copy-done | bytes 1048600
  20.4 0.0 copy-start.1
  20.4 1.2 %copy-done.1 = bf16[1,4096,128]{2,1,0:T(8,128)(2,1)S(1)} copy-done((bf16[1,4096,128]{2,1,0:T(8,128)(2,1)S(1)}, bf16[1,4096,128]{2,1,0:T(8,128)(2,1)}, u32[]{:S(2)}) %copy-start.1) | copy-done | bytes 1048600
  21.6 6.3 %shard_map.92 = bf16[128,512]{1,0:T(8,128)(2,1)S(1)} custom-call(s32[8]{0:T(128)S(1)} %copy-done.2, s32[8]{0:T(128)S(1)} %copy-done.3, s32[8]{0:T(128)S(1)} %copy-done.4, s32[8]{0:T(128)S(1)} %copy-done.5, bf16[128,768]{1,0:T(8,128)(2,1)S(1)} %bitcast.9, bf16[128,768]{1,0:T(8,128)(2,1)S(1)} %collective-permute-done.peer_ref, ...), custom_call_target="tpu_custom_call" | custom-call | tf_op jit(solution)/shard_map/pallas_call | solution.py:417
  28.0 10.6 %all_to_all.11.in_ref = bf16[8,16,512]{2,1,0:T(8,128)(2,1)} all-to-all(bf16[8,16,512]{2,1,0:T(8,128)(2,1)S(1)} %bitcast.10), channel_id=1, replica_groups=mesh['rep'=2,'head'=8,'seq'=2] {'head'}, dimensions={0} | all-to-all | bytes 262144 | tf_op jit(solution)/shard_map/all_to_all | solution.py:441
  38.6 1.6 %shard_map.93 = bf16[16,4096]{1,0:T(8,128)(2,1)} custom-call(s32[8]{0:T(128)} %head_ref.5, bf16[8,16,512]{2,1,0:T(8,128)(2,1)} %all_to_all.11.in_ref), custom_call_target="tpu_custom_call" | custom-call | tf_op jit(solution)/shard_map/pallas_call | solution.py:442
Async XLA Ops:
  0.0 19.1 %collective-permute-start.1 = (bf16[4096,128]{1,0:T(8,128)(2,1)}, bf16[4096,128]{1,0:T(8,128)(2,1)S(1)}, u32[]{:S(2)}, u32[]{:S(2)}) collective-permute-start(bf16[4096,128]{1,0:T(8,128)(2,1)} %bitcast.4), channel_id=1, source_target_pairs={{0,1},{1,0},{2,3},{3,2},{4,5},{5,4},{6,7},{7,6},{8,9},{9,8},{10,11... | collective-permute-start | bytes 3145736 | tf_op jit(solution)/shard_map/ppermute | solution.py:403
  0.5 18.7 %collective-permute-start.2 = (bf16[4096,128]{1,0:T(8,128)(2,1)}, bf16[4096,128]{1,0:T(8,128)(2,1)S(1)}, u32[]{:S(2)}, u32[]{:S(2)}) collective-permute-start(bf16[4096,128]{1,0:T(8,128)(2,1)} %bitcast.6), channel_id=1, source_target_pairs={{0,1},{1,0},{2,3},{3,2},{4,5},{5,4},{6,7},{7,6},{8,9},{9,8},{10,11... | collective-permute-start | bytes 3145736 | tf_op jit(solution)/shard_map/ppermute | solution.py:404
  2.1 17.0 %copy-start.5 = (s32[8]{0:T(128)S(1)}, s32[8]{0:T(128)}, u32[]{:S(2)}) copy-start(s32[8]{0:T(128)} %sink_ref.1) | copy-start | bytes 100
  17.7 1.5 %copy-start.2 = (s32[8]{0:T(128)S(1)}, s32[8]{0:T(128)}, u32[]{:S(2)}) copy-start(s32[8]{0:T(128)} %head_ref.5) | copy-start | bytes 100
  17.7 1.5 %copy-start.3 = (s32[8]{0:T(128)S(1)}, s32[8]{0:T(128)}, u32[]{:S(2)}) copy-start(s32[8]{0:T(128)} %retrieval_ref.1) | copy-start | bytes 100
  17.7 1.5 %copy-start.4 = (s32[8]{0:T(128)S(1)}, s32[8]{0:T(128)}, u32[]{:S(2)}) copy-start(s32[8]{0:T(128)} %window_ref.1) | copy-start | bytes 100
  17.7 1.4 %collective-permute-start = (bf16[128,768]{1,0:T(8,128)(2,1)S(1)}, bf16[128,768]{1,0:T(8,128)(2,1)S(1)}, u32[]{:S(2)}, u32[]{:S(2)}) collective-permute-start(bf16[128,768]{1,0:T(8,128)(2,1)S(1)} %bitcast.8), channel_id=1, source_target_pairs={{0,1},{1,0},{2,3},{3,2},{4,5},{5,4},{6,7},{7,6},{8,9},{9,8},{10,11... | collective-permute-start | bytes 589832 | tf_op jit(solution)/shard_map/ppermute | solution.py:413
  19.2 1.2 %copy-start = (bf16[1,4096,128]{2,1,0:T(8,128)(2,1)S(1)}, bf16[1,4096,128]{2,1,0:T(8,128)(2,1)}, u32[]{:S(2)}) copy-start(bf16[1,4096,128]{2,1,0:T(8,128)(2,1)} %param.12) | copy-start | bytes 3145732
  20.4 1.2 %copy-start.1 = (bf16[1,4096,128]{2,1,0:T(8,128)(2,1)S(1)}, bf16[1,4096,128]{2,1,0:T(8,128)(2,1)}, u32[]{:S(2)}) copy-start(bf16[1,4096,128]{2,1,0:T(8,128)(2,1)} %param.13) | copy-start | bytes 3145732

commit v2 on v1

--- a/solution.py
+++ b/solution.py
@@ -175,24 +175,48 @@
 
 
 VMEM_SPEC = pl.BlockSpec(memory_space=pltpu.VMEM)
+HBM_SPEC = pl.BlockSpec(memory_space=pltpu.HBM)
 SMEM_SPEC = pl.BlockSpec(memory_space=pltpu.SMEM)
 
 
-def pack_kernel(head_ref, q_ref, k_ref, v_ref, out_ref, *, group_width, head_dim):
+def pack_kernel(head_ref, q_ref, k_ref, v_ref, out_ref, sems, *, group_width, head_dim):
+    copies = []
     for slot in range(out_ref.shape[0]):
         group = head_ref[slot]
         q_start = pl.multiple_of(group * group_width, 128)
         kv_start = pl.multiple_of(group * head_dim, 128)
-        out_ref[slot, :, :group_width] = q_ref[:, pl.ds(q_start, group_width)]
-        out_ref[slot, :, group_width : group_width + head_dim] = k_ref[:, pl.ds(kv_start, head_dim)]
-        out_ref[slot, :, group_width + head_dim :] = v_ref[:, pl.ds(kv_start, head_dim)]
-
-
-def unpack_kernel(head_ref, in_ref, out_ref):
+        for part, (source, start, place, width) in enumerate(
+            (
+                (q_ref, q_start, 0, group_width),
+                (k_ref, kv_start, group_width, head_dim),
+                (v_ref, kv_start, group_width + head_dim, head_dim),
+            )
+        ):
+            copies.append(
+                pltpu.make_async_copy(
+                    source.at[:, pl.ds(start, width)],
+                    out_ref.at[slot, :, pl.ds(place, width)],
+                    sems.at[slot, part],
+                )
+            )
+    for copy in copies:
+        copy.start()
+    for copy in copies:
+        copy.wait()
+
+
+def unpack_kernel(head_ref, in_ref, out_ref, sems):
     width = in_ref.shape[2]
+    copies = []
     for slot in range(in_ref.shape[0]):
         start = pl.multiple_of(head_ref[slot] * width, 128)
-        out_ref[:, pl.ds(start, width)] = in_ref[slot]
+        copies.append(
+            pltpu.make_async_copy(in_ref.at[slot], out_ref.at[:, pl.ds(start, width)], sems.at[slot])
+        )
+    for copy in copies:
+        copy.start()
+    for copy in copies:
+        copy.wait()
 
 
 def attend_kernel(
@@ -405,8 +429,9 @@
     send = pl.pallas_call(
         functools.partial(pack_kernel, group_width=group_width, head_dim=head_dim),
         out_shape=jax.ShapeDtypeStruct((head_count, tok_rows, group_width + 2 * head_dim), jnp.bfloat16),
-        in_specs=[SMEM_SPEC, VMEM_SPEC, VMEM_SPEC, VMEM_SPEC],
-        out_specs=VMEM_SPEC,
+        in_specs=[SMEM_SPEC, HBM_SPEC, HBM_SPEC, HBM_SPEC],
+        out_specs=HBM_SPEC,
+        scratch_shapes=[pltpu.SemaphoreType.DMA((head_count, 3))],
     )(head_list, q_span, k_span, v_span)
     recv = lax.all_to_all(send, "head", split_axis=0, concat_axis=0, tiled=True)
     recv = recv.reshape(tokens, group_width + 2 * head_dim)
@@ -424,7 +449,7 @@
             row_block=row_block,
         ),
         out_shape=jax.ShapeDtypeStruct((tokens, group_width), jnp.bfloat16),
-        in_specs=[SMEM_SPEC] * 4 + [VMEM_SPEC] * 4 + [pl.BlockSpec(memory_space=pltpu.HBM)] * 2,
+        in_specs=[SMEM_SPEC] * 4 + [VMEM_SPEC] * 4 + [HBM_SPEC] * 2,
         out_specs=VMEM_SPEC,
         scratch_shapes=[
             pltpu.VMEM((ctx_dev, head_dim), jnp.bfloat16),
@@ -435,15 +460,16 @@
             pltpu.VMEM((head_dim, rows), jnp.float32),
             pltpu.SemaphoreType.DMA((2,)),
         ],
-        compiler_params=pltpu.CompilerParams(vmem_limit_bytes=40 * 2**20),
+        compiler_params=pltpu.CompilerParams(vmem_limit_bytes=51 * 2**20),
     )(head_list, retrieval, windows, sinks, recv, peer, k_peer, v_peer, k_own, v_own)
     result = result.reshape(head_count, tok_rows, group_width)
     back = lax.all_to_all(result, "head", split_axis=0, concat_axis=0, tiled=True)
     return pl.pallas_call(
         unpack_kernel,
         out_shape=jax.ShapeDtypeStruct((tok_rows, KVH * group_width), jnp.bfloat16),
-        in_specs=[SMEM_SPEC, VMEM_SPEC],
-        out_specs=VMEM_SPEC,
+        in_specs=[SMEM_SPEC, HBM_SPEC],
+        out_specs=HBM_SPEC,
+        scratch_shapes=[pltpu.SemaphoreType.DMA((head_count,))],
     )(head_list, back)
 
 

time: 40.5 us -> 49.2 us (1.21); the launches traced: 40.2 us -> 48.4 us
  Pallas kernels: 9.55 us -> 20.3 us
  local copies, waits for them, and re-layouts: 2.46 us -> 0.02 us
    pallas_call x1, Pallas kernels: 1.63 us -> 7.94 us  [on_device_pairs(): pl.pallas_call(functools.partial(pack_kernel, group_width=group_width, he...]
    pallas_call x1, Pallas kernels: 1.58 us -> 5.81 us  [on_device_pairs(): pl.pallas_call(unpack_kernel, out_shape=jax.ShapeDtypeStruct((tok_rows, K...]
    unnamed x12 -> x8, local copies, waits for them, and re-layouts: 2.46 us -> 0.02 us
  transfers between devices with their start and end apart: 3 -> 3, of which waited for: 1 -> 1; matrix products, arithmetic and copies ran while one was open for 0% -> 0% of each run, Pallas kernels for 4% -> 16%
where the time goes in v2:
time: 49.2 us; the launch traced here: 48.4 us
  blocking collectives  26.1 us (53%)
  Pallas kernels  20.3 us (41%)
  waiting for transfers between devices  1.44 us (3%)
  starting transfers between devices  0.51 us (1%)
    all_to_all x1, blocking collectives, on_device_pairs(): recv = lax.all_to_all(send, 'head', split_axis=0, concat_axis=0, tiled=True)  15.4 us
    all_to_all x1, blocking collectives, on_device_pairs(): lax.all_to_all(result, 'head', split_axis=0, concat_axis=0, tiled=True)  10.6 us
    pallas_call x1, Pallas kernels, on_device_pairs(): pl.pallas_call(functools.partial(pack_kernel, group_width=group_width, he...  7.94 us
    pallas_call x1, Pallas kernels, on_device_pairs(): pl.pallas_call(functools.partial(attend_kernel, tok_rows=tok_rows, group_...  6.53 us
    pallas_call x1, Pallas kernels, on_device_pairs(): pl.pallas_call(unpack_kernel, out_shape=jax.ShapeDtypeStruct((tok_rows, K...  5.81 us
    ppermute x1, waiting for transfers between devices, on_device_pairs(): peer = lax.ppermute(recv, 'seq', swap)  1.43 us
  transfers between devices with their start and end apart: 3, of which 1 were waited for; matrix products, arithmetic and copies ran while one was open for 0% of the time, Pallas kernels for 16%

profile of v2, /device:TPU:0, one launch (start us, length us, event | category | flops | bytes accessed | tf_op | source)
XLA Modules:
  0.0 48.4 jit_solution(15649678109229186469)
XLA Ops:
  0.0 0.5 collective-permute-start.1
  0.5 0.1 collective-permute-start.2
  0.5 7.9 %shard_map.91 = bf16[8,16,768]{2,1,0:T(8,128)(2,1)} custom-call(s32[8]{0:T(128)} %head_ref.5, bf16[16,4096]{1,0:T(8,128)(2,1)} %q_ref.1, bf16[16,1024]{1,0:T(8,128)(2,1)} %k_ref.1, bf16[16,1024]{1,0:T(8,128)(2,1)} %v_ref.1), custom_call_target="tpu_custom_call" | custom-call | tf_op jit(solution)/shard_map/pallas_call | solution.py:429
  8.5 0.0 copy-start.3
  8.5 15.4 %all_to_all.10 = bf16[8,16,768]{2,1,0:T(8,128)(2,1)S(1)} all-to-all(bf16[8,16,768]{2,1,0:T(8,128)(2,1)} %shard_map.91), channel_id=1, replica_groups=mesh['rep'=2,'head'=8,'seq'=2] {'head'}, dimensions={0} | all-to-all | bytes 393216 | tf_op jit(solution)/shard_map/all_to_all | solution.py:436
  23.9 0.0 copy-start
  23.9 0.0 copy-start.1
  23.9 0.0 copy-start.2
  23.9 0.0 collective-permute-start
  23.9 1.4 %collective-permute-done.peer_ref = bf16[128,768]{1,0:T(8,128)(2,1)S(1)} collective-permute-done((bf16[128,768]{1,0:T(8,128)(2,1)S(1)}, bf16[128,768]{1,0:T(8,128)(2,1)S(1)}, u32[]{:S(2)}, u32[]{:S(2)}) %collective-permute-start) | collective-permute-done | bytes 196640 | tf_op jit(solution)/shard_map/ppermute | solution.py:438
  25.3 0.0 collective-permute-done.1.k_peer
  25.3 0.0 collective-permute-done.2.v_peer
  25.3 0.0 copy-done.3
  25.3 0.0 copy-done
  25.4 0.0 copy-done.1
  25.4 0.0 copy-done.2
  25.4 6.5 %shard_map.92 = bf16[128,512]{1,0:T(8,128)(2,1)S(1)} custom-call(s32[8]{0:T(128)S(1)} %copy-done, s32[8]{0:T(128)S(1)} %copy-done.1, s32[8]{0:T(128)S(1)} %copy-done.2, s32[8]{0:T(128)S(1)} %copy-done.3, bf16[128,768]{1,0:T(8,128)(2,1)S(1)} %bitcast.5, bf16[128,768]{1,0:T(8,128)(2,1)S(1)} %collective-permute-done.peer_ref, ...), custom_call_target="tpu_custom_call" | custom-call | tf_op jit(solution)/shard_map/pallas_call | solution.py:442
  31.9 10.6 %all_to_all.11.in_ref = bf16[8,16,512]{2,1,0:T(8,128)(2,1)} all-to-all(bf16[8,16,512]{2,1,0:T(8,128)(2,1)S(1)} %bitcast.6), channel_id=1, replica_groups=mesh['rep'=2,'head'=8,'seq'=2] {'head'}, dimensions={0} | all-to-all | bytes 262144 | tf_op jit(solution)/shard_map/all_to_all | solution.py:466
  42.6 5.8 %shard_map.93 = bf16[16,4096]{1,0:T(8,128)(2,1)} custom-call(s32[8]{0:T(128)} %head_ref.5, bf16[8,16,512]{2,1,0:T(8,128)(2,1)} %all_to_all.11.in_ref), custom_call_target="tpu_custom_call" | custom-call | tf_op jit(solution)/shard_map/pallas_call | solution.py:467
Async XLA Ops:
  0.0 25.3 %collective-permute-start.1 = (bf16[4096,128]{1,0:T(8,128)(2,1)}, bf16[4096,128]{1,0:T(8,128)(2,1)S(1)}, u32[]{:S(2)}, u32[]{:S(2)}) collective-permute-start(bf16[4096,128]{1,0:T(8,128)(2,1)} %bitcast.7), channel_id=1, source_target_pairs={{0,1},{1,0},{2,3},{3,2},{4,5},{5,4},{6,7},{7,6},{8,9},{9,8},{10,11... | collective-permute-start | bytes 3145736 | tf_op jit(solution)/shard_map/ppermute | solution.py:427
  0.5 24.9 %collective-permute-start.2 = (bf16[4096,128]{1,0:T(8,128)(2,1)}, bf16[4096,128]{1,0:T(8,128)(2,1)S(1)}, u32[]{:S(2)}, u32[]{:S(2)}) collective-permute-start(bf16[4096,128]{1,0:T(8,128)(2,1)} %bitcast.9), channel_id=1, source_target_pairs={{0,1},{1,0},{2,3},{3,2},{4,5},{5,4},{6,7},{7,6},{8,9},{9,8},{10,11... | collective-permute-start | bytes 3145736 | tf_op jit(solution)/shard_map/ppermute | solution.py:428
  8.5 16.9 %copy-start.3 = (s32[8]{0:T(128)S(1)}, s32[8]{0:T(128)}, u32[]{:S(2)}) copy-start(s32[8]{0:T(128)} %sink_ref.1) | copy-start | bytes 100
  23.9 1.5 %copy-start = (s32[8]{0:T(128)S(1)}, s32[8]{0:T(128)}, u32[]{:S(2)}) copy-start(s32[8]{0:T(128)} %head_ref.5) | copy-start | bytes 100
  23.9 1.5 %copy-start.1 = (s32[8]{0:T(128)S(1)}, s32[8]{0:T(128)}, u32[]{:S(2)}) copy-start(s32[8]{0:T(128)} %retrieval_ref.1) | copy-start | bytes 100
  23.9 1.5 %copy-start.2 = (s32[8]{0:T(128)S(1)}, s32[8]{0:T(128)}, u32[]{:S(2)}) copy-start(s32[8]{0:T(128)} %window_ref.1) | copy-start | bytes 100
  23.9 1.4 %collective-permute-start = (bf16[128,768]{1,0:T(8,128)(2,1)S(1)}, bf16[128,768]{1,0:T(8,128)(2,1)S(1)}, u32[]{:S(2)}, u32[]{:S(2)}) collective-permute-start(bf16[128,768]{1,0:T(8,128)(2,1)S(1)} %bitcast.4), channel_id=1, source_target_pairs={{0,1},{1,0},{2,3},{3,2},{4,5},{5,4},{6,7},{7,6},{8,9},{9,8},{10,11... | collective-permute-start | bytes 589832 | tf_op jit(solution)/shard_map/ppermute | solution.py:438

commit v3 on v1

--- a/solution.py
+++ b/solution.py
@@ -175,6 +175,7 @@
 
 
 VMEM_SPEC = pl.BlockSpec(memory_space=pltpu.VMEM)
+HBM_SPEC = pl.BlockSpec(memory_space=pltpu.HBM)
 SMEM_SPEC = pl.BlockSpec(memory_space=pltpu.SMEM)
 
 
@@ -407,6 +408,7 @@
         out_shape=jax.ShapeDtypeStruct((head_count, tok_rows, group_width + 2 * head_dim), jnp.bfloat16),
         in_specs=[SMEM_SPEC, VMEM_SPEC, VMEM_SPEC, VMEM_SPEC],
         out_specs=VMEM_SPEC,
+        compiler_params=pltpu.CompilerParams(vmem_limit_bytes=2**20),
     )(head_list, q_span, k_span, v_span)
     recv = lax.all_to_all(send, "head", split_axis=0, concat_axis=0, tiled=True)
     recv = recv.reshape(tokens, group_width + 2 * head_dim)
@@ -424,7 +426,7 @@
             row_block=row_block,
         ),
         out_shape=jax.ShapeDtypeStruct((tokens, group_width), jnp.bfloat16),
-        in_specs=[SMEM_SPEC] * 4 + [VMEM_SPEC] * 4 + [pl.BlockSpec(memory_space=pltpu.HBM)] * 2,
+        in_specs=[SMEM_SPEC] * 4 + [VMEM_SPEC] * 4 + [HBM_SPEC] * 2,
         out_specs=VMEM_SPEC,
         scratch_shapes=[
             pltpu.VMEM((ctx_dev, head_dim), jnp.bfloat16),
@@ -435,7 +437,7 @@
             pltpu.VMEM((head_dim, rows), jnp.float32),
             pltpu.SemaphoreType.DMA((2,)),
         ],
-        compiler_params=pltpu.CompilerParams(vmem_limit_bytes=40 * 2**20),
+        compiler_params=pltpu.CompilerParams(vmem_limit_bytes=51 * 2**20),
     )(head_list, retrieval, windows, sinks, recv, peer, k_peer, v_peer, k_own, v_own)
     result = result.reshape(head_count, tok_rows, group_width)
     back = lax.all_to_all(result, "head", split_axis=0, concat_axis=0, tiled=True)
@@ -444,6 +446,7 @@
         out_shape=jax.ShapeDtypeStruct((tok_rows, KVH * group_width), jnp.bfloat16),
         in_specs=[SMEM_SPEC, VMEM_SPEC],
         out_specs=VMEM_SPEC,
+        compiler_params=pltpu.CompilerParams(vmem_limit_bytes=2**20),
     )(head_list, back)
 
 

time: 40.5 us -> 39.2 us (0.968)
  blocking collectives: 26.2 us -> 25.1 us
    pallas_call x1, Pallas kernels: 6.33 us -> 7.67 us  [on_device_pairs(): pl.pallas_call(functools.partial(attend_kernel, tok_rows=tok_rows, group_...]
    pallas_call x1, Pallas kernels: 1.63 us -> 0.57 us  [on_device_pairs(): pl.pallas_call(functools.partial(pack_kernel, group_width=group_width, he...]
    all_to_all x1, blocking collectives: 10.6 us -> 9.96 us  [on_device_pairs(): lax.all_to_all(result, 'head', split_axis=0, concat_axis=0, tiled=True)]
    all_to_all x1, blocking collectives: 15.5 us -> 15.1 us  [on_device_pairs(): recv = lax.all_to_all(send, 'head', split_axis=0, concat_axis=0, tiled=True)]
    unnamed x12 -> x14, local copies, waits for them, and re-layouts: 2.46 us -> 2.57 us
  transfers between devices with their start and end apart: 3 -> 3, of which waited for: 1 -> 1; matrix products, arithmetic and copies ran while one was open for 0% -> 0% of each run, Pallas kernels for 4% -> 1%
where the time goes in v3:
time: 39.2 us; the launch traced here: 39.1 us
  blocking collectives  25.1 us (64%)
  Pallas kernels  9.45 us (24%)
  local copies, waits for them, and re-layouts  2.57 us (7%)
  waiting for transfers between devices  1.44 us (4%)
  starting transfers between devices  0.52 us (1%)
    all_to_all x1, blocking collectives, on_device_pairs(): recv = lax.all_to_all(send, 'head', split_axis=0, concat_axis=0, tiled=True)  15.1 us
    all_to_all x1, blocking collectives, on_device_pairs(): lax.all_to_all(result, 'head', split_axis=0, concat_axis=0, tiled=True)  9.96 us
    pallas_call x1, Pallas kernels, on_device_pairs(): pl.pallas_call(functools.partial(attend_kernel, tok_rows=tok_rows, group_...  7.67 us
    unnamed x14, local copies, waits for them, and re-layouts  2.57 us
    ppermute x1, waiting for transfers between devices, on_device_pairs(): peer = lax.ppermute(recv, 'seq', swap)  1.43 us
    pallas_call x1, Pallas kernels, on_device_pairs(): pl.pallas_call(unpack_kernel, out_shape=jax.ShapeDtypeStruct((tok_rows, K...  1.21 us
  transfers between devices with their start and end apart: 3, of which 1 were waited for; matrix products, arithmetic and copies ran while one was open for 0% of the time, Pallas kernels for 1%

profile of v3, /device:TPU:0, one launch (start us, length us, event | category | flops | bytes accessed | tf_op | source)
XLA Modules:
  0.0 39.1 jit_solution(10896236210532055941)
XLA Ops:
  0.0 0.0 copy-start.3
  0.0 0.5 %collective-permute-start.1 = (bf16[4096,128]{1,0:T(8,128)(2,1)}, bf16[4096,128]{1,0:T(8,128)(2,1)S(1)}, u32[]{:S(2)}, u32[]{:S(2)}) collective-permute-start(bf16[4096,128]{1,0:T(8,128)(2,1)} %bitcast.7), channel_id=1, source_target_pairs={{0,1},{1,0},{2,3},{3,2},{4,5},{5,4},{6,7},{7,6},{8,9},{9,8},{10,11... | collective-permute-start | bytes 3145736 | tf_op jit(solution)/shard_map/ppermute | solution.py:404
  0.5 0.1 collective-permute-start.2
  0.5 0.1 copy-done.3
  0.7 0.0 copy-start
  0.7 0.9 %copy-done = bf16[16,4096]{1,0:T(8,128)(2,1)S(1)} copy-done((bf16[16,4096]{1,0:T(8,128)(2,1)S(1)}, bf16[16,4096]{1,0:T(8,128)(2,1)}, u32[]{:S(2)}) %copy-start) | copy-done | bytes 131096
  1.6 0.0 copy-start.1
  1.6 0.8 %copy-done.1 = bf16[16,1024]{1,0:T(8,128)(2,1)S(1)} copy-done((bf16[16,1024]{1,0:T(8,128)(2,1)S(1)}, bf16[16,1024]{1,0:T(8,128)(2,1)}, u32[]{:S(2)}) %copy-start.1) | copy-done | bytes 32792
  2.3 0.0 copy-start.2
  2.3 0.8 %copy-done.2 = bf16[16,1024]{1,0:T(8,128)(2,1)S(1)} copy-done((bf16[16,1024]{1,0:T(8,128)(2,1)S(1)}, bf16[16,1024]{1,0:T(8,128)(2,1)}, u32[]{:S(2)}) %copy-start.2) | copy-done | bytes 32792
  3.1 0.6 %shard_map.91 = bf16[8,16,768]{2,1,0:T(8,128)(2,1)S(1)} custom-call(s32[8]{0:T(128)S(1)} %copy-done.3, bf16[16,4096]{1,0:T(8,128)(2,1)S(1)} %copy-done, bf16[16,1024]{1,0:T(8,128)(2,1)S(1)} %copy-done.1, bf16[16,1024]{1,0:T(8,128)(2,1)S(1)} %copy-done.2), custom_call_target="tpu_custom_call" | custom-call | tf_op jit(solution)/shard_map/pallas_call | solution.py:406
  3.7 15.1 %all_to_all.10 = bf16[8,16,768]{2,1,0:T(8,128)(2,1)S(1)} all-to-all(bf16[8,16,768]{2,1,0:T(8,128)(2,1)S(1)} %shard_map.91), channel_id=1, replica_groups=mesh['rep'=2,'head'=8,'seq'=2] {'head'}, dimensions={0} | all-to-all | bytes 393216 | tf_op jit(solution)/shard_map/all_to_all | solution.py:413
  18.8 0.0 copy-start.4
  18.8 0.0 copy-start.5
  18.8 0.0 copy-start.6
  18.8 0.0 collective-permute-start
  18.8 1.4 %collective-permute-done.peer_ref = bf16[128,768]{1,0:T(8,128)(2,1)S(1)} collective-permute-done((bf16[128,768]{1,0:T(8,128)(2,1)S(1)}, bf16[128,768]{1,0:T(8,128)(2,1)S(1)}, u32[]{:S(2)}, u32[]{:S(2)}) %collective-permute-start) | collective-permute-done | bytes 196640 | tf_op jit(solution)/shard_map/ppermute | solution.py:415
  20.2 0.0 collective-permute-done.1.k_peer
  20.2 0.0 collective-permute-done.2.v_peer
  20.2 0.0 copy-done.4
  20.2 0.0 copy-done.5
  20.2 0.0 copy-done.6
  20.3 7.7 %shard_map.92 = bf16[128,512]{1,0:T(8,128)(2,1)S(1)} custom-call(s32[8]{0:T(128)S(1)} %copy-done.3, s32[8]{0:T(128)S(1)} %copy-done.4, s32[8]{0:T(128)S(1)} %copy-done.5, s32[8]{0:T(128)S(1)} %copy-done.6, bf16[128,768]{1,0:T(8,128)(2,1)S(1)} %bitcast.5, bf16[128,768]{1,0:T(8,128)(2,1)S(1)} %collective-permute-done.peer_ref, ...), custom_call_target="tpu_custom_call" | custom-call | tf_op jit(solution)/shard_map/pallas_call | solution.py:419
  27.9 10.0 %all_to_all.11.in_ref = bf16[8,16,512]{2,1,0:T(8,128)(2,1)S(1)} all-to-all(bf16[8,16,512]{2,1,0:T(8,128)(2,1)S(1)} %bitcast.6), channel_id=1, replica_groups=mesh['rep'=2,'head'=8,'seq'=2] {'head'}, dimensions={0} | all-to-all | bytes 262144 | tf_op jit(solution)/shard_map/all_to_all | solution.py:443
  37.9 1.2 %shard_map.93 = bf16[16,4096]{1,0:T(8,128)(2,1)} custom-call(s32[8]{0:T(128)S(1)} %copy-done.3, bf16[8,16,512]{2,1,0:T(8,128)(2,1)S(1)} %all_to_all.11.in_ref), custom_call_target="tpu_custom_call" | custom-call | tf_op jit(solution)/shard_map/pallas_call | solution.py:444
Async XLA Ops:
  0.0 0.7 %copy-start.3 = (s32[8]{0:T(128)S(1)}, s32[8]{0:T(128)}, u32[]{:S(2)}) copy-start(s32[8]{0:T(128)} %head_ref.5) | copy-start | bytes 100
  0.0 20.2 %collective-permute-start.1 = (bf16[4096,128]{1,0:T(8,128)(2,1)}, bf16[4096,128]{1,0:T(8,128)(2,1)S(1)}, u32[]{:S(2)}, u32[]{:S(2)}) collective-permute-start(bf16[4096,128]{1,0:T(8,128)(2,1)} %bitcast.7), channel_id=1, source_target_pairs={{0,1},{1,0},{2,3},{3,2},{4,5},{5,4},{6,7},{7,6},{8,9},{9,8},{10,11... | collective-permute-start | bytes 3145736 | tf_op jit(solution)/shard_map/ppermute | solution.py:404
  0.5 19.8 %collective-permute-start.2 = (bf16[4096,128]{1,0:T(8,128)(2,1)}, bf16[4096,128]{1,0:T(8,128)(2,1)S(1)}, u32[]{:S(2)}, u32[]{:S(2)}) collective-permute-start(bf16[4096,128]{1,0:T(8,128)(2,1)} %bitcast.9), channel_id=1, source_target_pairs={{0,1},{1,0},{2,3},{3,2},{4,5},{5,4},{6,7},{7,6},{8,9},{9,8},{10,11... | collective-permute-start | bytes 3145736 | tf_op jit(solution)/shard_map/ppermute | solution.py:405
  0.7 0.9 %copy-start = (bf16[16,4096]{1,0:T(8,128)(2,1)S(1)}, bf16[16,4096]{1,0:T(8,128)(2,1)}, u32[]{:S(2)}) copy-start(bf16[16,4096]{1,0:T(8,128)(2,1)} %q_ref.1) | copy-start | bytes 393220
  1.6 0.8 %copy-start.1 = (bf16[16,1024]{1,0:T(8,128)(2,1)S(1)}, bf16[16,1024]{1,0:T(8,128)(2,1)}, u32[]{:S(2)}) copy-start(bf16[16,1024]{1,0:T(8,128)(2,1)} %k_ref.1) | copy-start | bytes 98308
  2.3 0.8 %copy-start.2 = (bf16[16,1024]{1,0:T(8,128)(2,1)S(1)}, bf16[16,1024]{1,0:T(8,128)(2,1)}, u32[]{:S(2)}) copy-start(bf16[16,1024]{1,0:T(8,128)(2,1)} %v_ref.1) | copy-start | bytes 98308
  18.8 1.5 %copy-start.4 = (s32[8]{0:T(128)S(1)}, s32[8]{0:T(128)}, u32[]{:S(2)}) copy-start(s32[8]{0:T(128)} %retrieval_ref.1) | copy-start | bytes 100
  18.8 1.5 %copy-start.5 = (s32[8]{0:T(128)S(1)}, s32[8]{0:T(128)}, u32[]{:S(2)}) copy-start(s32[8]{0:T(128)} %window_ref.1) | copy-start | bytes 100
  18.8 1.5 %copy-start.6 = (s32[8]{0:T(128)S(1)}, s32[8]{0:T(128)}, u32[]{:S(2)}) copy-start(s32[8]{0:T(128)} %sink_ref.1) | copy-start | bytes 100
  18.8 1.4 %collective-permute-start = (bf16[128,768]{1,0:T(8,128)(2,1)S(1)}, bf16[128,768]{1,0:T(8,128)(2,1)S(1)}, u32[]{:S(2)}, u32[]{:S(2)}) collective-permute-start(bf16[128,768]{1,0:T(8,128)(2,1)S(1)} %bitcast.4), channel_id=1, source_target_pairs={{0,1},{1,0},{2,3},{3,2},{4,5},{5,4},{6,7},{7,6},{8,9},{9,8},{10,11... | collective-permute-start | bytes 589832 | tf_op jit(solution)/shard_map/ppermute | solution.py:415
